TPU v7x, 256 devices: a whole 4x4x8 slice. The times are simulated.
256 devices in a mesh: rows: 16 (over y, x), feat: 16 (over z, core).
Axes of the slice: x: 4, y: 4, z: 8, core: 2. Of those that a mesh axis runs over, the one named last changes fastest.
Arguments:
- feature_bins: int32 [512, 131072], P('feat', 'rows'), may hold values from 0 to 127
- leaf_index: int32 [131072], P('rows'), may hold values from 0 to 63
- doc_scores: float32 [131072], P('rows'), may hold values from -8 to 256
- doc_weights: float32 [131072], P('rows'), may hold values from 0.3 to 3
- destination: int32 [131072], P('rows'), may hold values from 0 to 131071, as said below
- query_ids: int32 [131072], P('rows'), may hold values from 0 to 131071, as said below
- clicks: int32 [131072], P('rows'), may hold values 0 or 1
Outputs:
- histograms: float32 [64, 512, 2, 128], P('rows', 'feat')
Inputs may be any that keep to these rules, and one draw needn't show every extreme that they name: A permutation of the slots; document i goes to owner destination // 8192, slot destination % 8192; each device's 8192 documents hold exactly 512 for every owner. `query_ids`: a query's id is the number of its last slot; each query's slots are consecutive, lie in one aligned block of 256 slots and hold 1 to 256 slots; every owner's slots hold a query of exactly 256.
All inputs are finite; a program needn't handle non-finite values. No bound on the sum of `clicks` on one device may be relied on, other than what follows from the above.
Results may differ from a plain program's by a relative error of at most 0.0023.
Values may be sent and summed in bfloat16 or wider, within the bound.
No kernel may reach another device: no remote copies, remote signals or barrier semaphores. Data moves between devices by JAX's collectives and lax.ppermute only.
A program may use at most 64 MiB of HBM per device.

v0:
```python
import math
import jax
import jax.numpy as jnp
from jax import lax
from jax.sharding import PartitionSpec as P

BINS = 128
LEAVES = 64
QBLOCK = 256


def block_gradients(approx, weight, query_block, target):
    same_query = query_block[:, None] == query_block[None, :]
    query_top = jnp.max(jnp.where(same_query, approx[None, :], -jnp.inf), axis=1)
    scaled = weight * jnp.exp(approx - query_top)
    matrix = same_query.astype(jnp.float32)
    denominator = jnp.dot(matrix, scaled, precision=lax.Precision.HIGHEST)
    clicked = jnp.dot(matrix, weight * target, precision=lax.Precision.HIGHEST)
    chance = scaled / denominator
    gradient = (weight * target - clicked * chance).astype(jnp.bfloat16)
    curvature = (clicked * chance * (1.0 - chance)).astype(jnp.bfloat16)
    return (gradient, curvature)


def query_gradients(approx, weight, query_ids, clicks):
    doc_count = approx.shape[0]
    nblocks = doc_count // QBLOCK
    per_step = 2
    shaped = lambda arr: arr.reshape(nblocks // per_step, per_step, QBLOCK)
    target = clicks.astype(jnp.float32)

    def step_blocks(inputs):
        return jax.vmap(block_gradients)(*inputs)

    gradient, curvature = lax.map(
        step_blocks, (shaped(approx), shaped(weight), shaped(query_ids), shaped(target))
    )
    return jnp.stack([gradient.reshape(doc_count), curvature.reshape(doc_count)])


def shards(feature_bins, leaf_index, doc_scores, doc_weights, destination, query_ids, clicks):
    owners = lax.axis_size("rows")
    doc_count = destination.shape[0]
    capacity = doc_count // owners
    ranking = jnp.argsort(destination)
    sorted_dest = destination[ranking]
    values = jnp.stack([doc_scores[ranking], doc_weights[ranking]]).reshape(2, owners, capacity)
    slot_ids = (sorted_dest % doc_count).reshape(owners, capacity)
    arrived = lax.all_to_all(values, "rows", split_axis=1, concat_axis=1, tiled=True)
    slot_in = lax.all_to_all(slot_ids, "rows", split_axis=0, concat_axis=0, tiled=True)
    owner_values = (
        jnp.zeros((2, doc_count), jnp.float32)
        .at[:, slot_in.reshape(-1)]
        .set(arrived.reshape(2, doc_count))
    )
    owner_stats = query_gradients(owner_values[0], owner_values[1], query_ids, clicks)
    outgoing = owner_stats[:, slot_in]
    returned = lax.all_to_all(outgoing, "rows", split_axis=1, concat_axis=1, tiled=True)
    doc_stats = (
        jnp.zeros((2, doc_count), jnp.bfloat16).at[:, ranking].set(returned.reshape(2, doc_count))
    )
    stats_rows = doc_stats.T
    f_dev = feature_bins.shape[0]
    bunch_size = math.gcd(4, f_dev)
    columns = feature_bins.reshape(f_dev // bunch_size, bunch_size, doc_count)
    bin_range = jnp.arange(BINS, dtype=jnp.int32)
    share = LEAVES // owners
    leaf_hot = (leaf_index[:, None] == jnp.arange(LEAVES, dtype=jnp.int32)[None, :]).astype(
        jnp.bfloat16
    )
    spread = (leaf_hot[:, :, None] * stats_rows[:, None, :]).reshape(doc_count, LEAVES * 2)

    def per_bunch(bunch):
        one_hot = (bunch[:, :, None] == bin_range).astype(jnp.bfloat16)
        return jnp.einsum("gdb,dk->gkb", one_hot, spread, preferred_element_type=jnp.float32)

    pieces = lax.map(per_bunch, columns).reshape(f_dev, LEAVES, 2, BINS)
    summed = lax.psum(jnp.transpose(pieces, (1, 0, 2, 3)), "rows")
    return lax.dynamic_slice_in_dim(summed, lax.axis_index("rows") * share, share, 0)


def solution(mesh):
    placed = (P("feat", "rows"), P("rows"), P("rows"), P("rows"), P("rows"), P("rows"), P("rows"))
    return jax.shard_map(
        shards, mesh=mesh, in_specs=placed, out_specs=P("rows", "feat", None, None), check_vma=False
    )
```

profile of v0, /device:TPU:2, one launch (start us, length us, event | category | flops | bytes accessed | tf_op | source)
XLA Modules:
  0.0 488.9 jit_solution(7182979089565845534)
XLA Ops:
  6.5 7.6 %sort.17 = (s32[8192]{0:T(1024)}, s32[8192]{0:T(1024)S(1)}) sort(s32[8192]{0:T(1024)} %param.15, s32[8192]{0:T(1024)S(1)} %iota.15), dimensions={0}, to_apply=%region_0.0 | sort | flops 106496 | bytes 131072 | tf_op jit(solution)/shard_map/jit(argsort)/sort | solution.py:45
  14.2 45.5 %gather_fusion = s32[8192]{0:T(1024)S(1)} fusion(s32[8192]{0:T(1024)S(1)} %copy-done.1, s32[8192]{0:T(1024)S(1)} %get-tuple-element.140), kind=kCustom, calls=%fused_computation | custom fusion | bytes 98304 | tf_op jit(solution)/shard_map/gather | solution.py:46
  60.4 7.5 %all-to-all-start = ((s32[16,1,512]{2,1,0:T(1,128)}), s32[16,1,512]{2,1,0:T(1,128)S(1)}, u32[]{:S(2)}, u32[]{:S(2)}) async-start(s32[16,1,512]{2,1,0:T(1,128)} %and_select_fusion), calls=%async_computation | async-start | bytes 65536 | tf_op jit(solution)/shard_map/all_to_all | solution.py:50
  67.9 45.5 %gather_fusion.1 = f32[8192]{0:T(1024)S(1)} fusion(f32[8192]{0:T(1024)S(1)} %copy-done, s32[8192]{0:T(1024)S(1)} %get-tuple-element.140), kind=kCustom, calls=%fused_computation.1 | custom fusion | bytes 98304 | tf_op jit(solution)/shard_map/gather | solution.py:47
  114.2 45.5 %gather_fusion.2 = f32[8192]{0:T(1024)S(1)} fusion(f32[8192]{0:T(1024)S(1)} %copy-done.2, s32[8192]{0:T(1024)S(1)} %get-tuple-element.140), kind=kCustom, calls=%fused_computation.2 | custom fusion | bytes 98304 | tf_op jit(solution)/shard_map/gather | solution.py:47
  160.5 7.2 %all-to-all-start.1 = ((f32[2,16,512]{2,0,1:T(2,128)}), f32[2,16,512]{2,0,1:T(2,128)S(1)}, u32[]{:S(2)}, u32[]{:S(2)}) async-start(f32[2,16,512]{2,0,1:T(2,128)} %copy.32), calls=%async_computation.1 | async-start | bytes 131072 | tf_op jit(solution)/shard_map/all_to_all | solution.py:49
  167.9 6.2 %all-to-all-done.1 = f32[2,16,512]{2,0,1:T(2,128)S(1)} async-done(((f32[2,16,512]{2,0,1:T(2,128)}), f32[2,16,512]{2,0,1:T(2,128)S(1)}, u32[]{:S(2)}, u32[]{:S(2)}) %all-to-all-start.1) | async-done | bytes 65568 | tf_op jit(solution)/shard_map/all_to_all | solution.py:49
  176.7 23.0 %scatter_custom_fusion = f32[2,8192]{0,1:T(8,128)} fusion(s32[8192]{0:T(1024)S(1)} %bitcast.107, f32[8192,2]{1,0:T(8,128)} %copy.33, f32[]{:T(128)} %constant.54.clone.1), kind=kCustom, calls=%fused_computation.44 | custom fusion | bytes 66048 | tf_op jit(solution)/shard_map/scatter | solution.py:54
  199.7 6.8 %slice_reduce_fusion = (f32[8192]{0:T(1024)S(1)}, f32[8192]{0:T(1024)S(1)}) fusion(f32[2,8192]{0,1:T(8,128)} %scatter_custom_fusion), kind=kLoop, calls=%fused_computation.42 | loop fusion | bytes 131072 | tf_op jit(solution)/shard_map/slice | solution.py:56
  206.5 18.5 %while.23 = (s32[]{:T(128)}, bf16[16,2,256]{2,1,0:T(2,128)(2,1)S(1)}, bf16[16,2,256]{2,1,0:T(2,128)(2,1)S(1)}, f32[16,2,256]{2,1,0:T(2,128)S(1)}, f32[16,2,256]{...) while((s32[]{:T(128)}, bf16[16,2,256]{2,1,0:T(2,128)(2,1)S(1)}, ...), condition=%wide.region_4.5_spmd, body=%wide.region_2.4_spmd.sunk | while | flops 3806722 | bytes 57449 | solution.py:35
  226.3 29.2 %gather_fusion.3 = bf16[8192,2]{1,0:T(8,128)(2,1)} fusion(bf16[2,8192]{0,1:T(8,128)(2,1)S(1)} %copy.34, s32[8192]{0:T(1024)S(1)} %broadcast_clamp_fusion), kind=kCustom, calls=%fused_computation.3 | custom fusion | bytes 98304 | tf_op jit(solution)/shard_map/gather | solution.py:57
  258.2 4.7 all-to-all-start.2
  264.4 4.8 all-to-all-done.2
  271.0 22.1 %scatter_custom_fusion.1 = bf16[2,8192]{0,1:T(8,128)(2,1)S(1)} fusion(s32[8192]{0:T(1024)S(1)} %get-tuple-element.141, bf16[8192,2]{1,0:T(8,128)(2,1)} %copy.36, bf16[]{:T(256)} %constant.55.clone.1), kind=kCustom, calls=%fused_computation.48 | custom fusion | bytes 33280 | tf_op jit(solution)/shard_map/scatter | solution.py:60
  294.1 85.1 %while.24 = (s32[]{:T(128)}, f32[8,4,128,128]{3,2,1,0:T(8,128)}, s32[8,4,8192]{2,1,0:T(4,128)}, bf16[8192,2]{0,1:T(2,128)(2,1)S(1)}, bf16[8192,64]{0,1:T(8,128)(2,1)S(1)}, /*index=5*/s32[]{:T(128)}) while((s32[]{:T(128)}, f32[8,4,128,128]{3,2,1,0:T(8,128)}, s32[8,4,8192]{2,1,0:T(4,128)}, bf16[8192,2]{0,1:T(2,128)(2,1)S(1)}, ...), condition=%wide.region_7.8_spmd.clone, body=%wide.region_6.7_spmd.clone.sunk | while | flops 1078984704 | bytes 11174473 | solution.py:77
  299.5 4.4 fusion.47
  310.1 4.4 fusion.47
  320.7 4.4 fusion.47
  331.4 4.4 fusion.47
  342.0 4.4 fusion.47
  352.6 4.4 fusion.47
  363.3 4.4 fusion.47
  373.9 4.4 fusion.47
  379.2 101.2 %all-reduce.2.cloned.1.call-done = f32[64,32,2,128]{3,2,0,1:T(2,128)} async-done(((f32[64,32,2,128]{3,2,0,1:T(2,128)}), f32[64,32,2,128]{3,2,0,1:T(2,128)}) %all-reduce.2.cloned.1.call-update) | async-done | bytes 2097168 | tf_op jit(solution)/shard_map/psum | solution.py:78
  (215 shorter events, 82.3 us)
Async XLA Ops:
  6.5 61.3 %copy-start = (f32[8192]{0:T(1024)S(1)}, f32[8192]{0:T(1024)}, u32[]{:S(2)}) copy-start(f32[8192]{0:T(1024)} %param.13) | copy-start | bytes 98308
  6.5 7.6 %copy-start.1 = (s32[8192]{0:T(1024)S(1)}, s32[8192]{0:T(1024)}, u32[]{:S(2)}) copy-start(s32[8192]{0:T(1024)} %param.15) | copy-start | bytes 98308
  60.4 100.1 %all-to-all-start = ((s32[16,1,512]{2,1,0:T(1,128)}), s32[16,1,512]{2,1,0:T(1,128)S(1)}, u32[]{:S(2)}, u32[]{:S(2)}) async-start(s32[16,1,512]{2,1,0:T(1,128)} %and_select_fusion), calls=%async_computation | async-start | bytes 65536 | tf_op jit(solution)/shard_map/all_to_all | solution.py:50
  113.4 0.8 copy-start.2
  114.2 46.3 %copy-start.5 = (s32[8192]{0:T(1024)S(1)}, s32[8192]{0:T(1024)}, u32[]{:S(2)}) copy-start(s32[8192]{0:T(1024)} %param.17) | copy-start | bytes 98308
  114.2 46.3 %copy-start.6 = (s32[8192]{0:T(1024)S(1)}, s32[8192]{0:T(1024)}, u32[]{:S(2)}) copy-start(s32[8192]{0:T(1024)} %param.16) | copy-start | bytes 98308
  160.5 13.5 %all-to-all-start.1 = ((f32[2,16,512]{2,0,1:T(2,128)}), f32[2,16,512]{2,0,1:T(2,128)S(1)}, u32[]{:S(2)}, u32[]{:S(2)}) async-start(f32[2,16,512]{2,0,1:T(2,128)} %copy.32), calls=%async_computation.1 | async-start | bytes 131072 | tf_op jit(solution)/shard_map/all_to_all | solution.py:49
  225.2 37.7 %copy-start.4 = (s32[8192]{0:T(1024)S(1)}, s32[8192]{0:T(1024)}, u32[]{:S(2)}) copy-start(s32[8192]{0:T(1024)} %param.12) | copy-start | bytes 98308
  226.3 36.9 %copy-start.3 = (s32[32,8192]{1,0:T(8,128)S(1)}, s32[32,8192]{1,0:T(8,128)}, u32[]{:S(2)}) copy-start(s32[32,8192]{1,0:T(8,128)} %param.11) | copy-start | bytes 3145732
  258.2 11.0 %all-to-all-start.2 = ((bf16[2,16,512]{2,0,1:T(2,128)(2,1)}), bf16[2,16,512]{2,0,1:T(2,128)(2,1)S(1)}, u32[]{:S(2)}, u32[]{:S(2)}) async-start(bf16[2,16,512]{2,0,1:T(2,128)(2,1)} %bitcast.18), calls=%async_computation.2 | async-start | bytes 65536 | tf_op jit(solution)/shard_map/all_to_all | solution.py:58
  262.9 217.5 %all-reduce.2.cloned.1.call-start = ((), (), s32[]{:S(2)}) async-start(), calls=%async_computation.3 | async-start | bytes 4194304 | tf_op jit(solution)/shard_map/psum | solution.py:78
Sparse Core Ops, SparseCore 0:
  379.3 101.0 all-reduce.1
where the time goes:
time: 490 us; the launch traced here: 489 us
  local copies, waits for them, and re-layouts  264 us (54%)
  waiting for transfers between devices  112 us (23%)
  matrix products  47.3 us (10%)
  other arithmetic  31.6 us (6%)
  starting transfers between devices  19.5 us (4%)
  between operations  13.7 us (3%)
    psum x1, waiting for transfers between devices, shards(): summed = lax.psum(jnp.transpose(pieces, (1, 0, 2, 3)), 'rows')  101 us
    gather x1, local copies, waits for them, and re-layouts, shards(): sorted_dest = destination[ranking]  45.5 us
    gather x1, local copies, waits for them, and re-layouts, shards(): doc_scores[ranking]  45.5 us
    gather x1, local copies, waits for them, and re-layouts, shards(): doc_weights[ranking]  45.5 us
    dot_general x8, matrix products, per_bunch(): jnp.einsum('gdb,dk->gkb', one_hot, spread, preferred_element_type=jnp.flo...  35 us
    gather x2, local copies, waits for them, and re-layouts, shards(): outgoing = owner_stats[:, slot_in]  31.8 us
    scatter x1, local copies, waits for them, and re-layouts, shards(): owner_values = jnp.zeros((2, doc_count), jnp.float32).at[:, slot_in.resha...  23 us
    scatter x1, local copies, waits for them, and re-layouts, shards(): jnp.zeros((2, doc_count), jnp.bfloat16).at[:, ranking]  22.1 us
  transfers between devices with their start and end apart: 4, of which 3 were waited for; matrix products, arithmetic and copies ran while one was open for 19% of the time, Pallas kernels for 0%

commit v1 on v0

--- a/solution.py
+++ b/solution.py
@@ -7,6 +7,12 @@
 BINS = 128
 LEAVES = 64
 QBLOCK = 256
+
+
+def summed_here(x, axis):
+    pieces = lax.all_gather(x, axis, axis=0, tiled=False)
+    acc = pieces.sum(axis=0)
+    return acc
 
 
 def block_gradients(approx, weight, query_block, target):
@@ -75,7 +81,7 @@
         return jnp.einsum("gdb,dk->gkb", one_hot, spread, preferred_element_type=jnp.float32)
 
     pieces = lax.map(per_bunch, columns).reshape(f_dev, LEAVES, 2, BINS)
-    summed = lax.psum(jnp.transpose(pieces, (1, 0, 2, 3)), "rows")
+    summed = summed_here(jnp.transpose(pieces, (1, 0, 2, 3)), "rows")
     return lax.dynamic_slice_in_dim(summed, lax.axis_index("rows") * share, share, 0)
 
 

time: 490 us -> 603 us (1.23)
  waiting for transfers between devices: 112 us -> 213 us
  other arithmetic: 31.6 us -> 44.4 us
    all_gather x0 -> x1, waiting for transfers between devices: none -> 202 us  [summed_here(): pieces = lax.all_gather(x, axis, axis=0, tiled=False)]
    psum x1 -> x0, waiting for transfers between devices: 101 us -> none  [shards(): summed = lax.psum(jnp.transpose(pieces, (1, 0, 2, 3)), 'rows')]
    reduce_sum x0 -> x1, other arithmetic: none -> 12.8 us  [summed_here(): acc = pieces.sum(axis=0)]
  transfers between devices with their start and end apart: 4 -> 4, of which waited for: 3 -> 3; matrix products, arithmetic and copies ran while one was open for 19% -> 16% of each run, Pallas kernels for 0% -> 0%
where the time goes in v1:
time: 603 us; the launch traced here: 602 us
  local copies, waits for them, and re-layouts  263 us (44%)
  waiting for transfers between devices  213 us (35%)
  matrix products  47.3 us (8%)
  other arithmetic  44.4 us (7%)
  starting transfers between devices  19.5 us (3%)
  between operations  13.7 us (2%)
    all_gather x1, waiting for transfers between devices, summed_here(): pieces = lax.all_gather(x, axis, axis=0, tiled=False)  202 us
    gather x1, local copies, waits for them, and re-layouts, shards(): sorted_dest = destination[ranking]  45.5 us
    gather x1, local copies, waits for them, and re-layouts, shards(): doc_scores[ranking]  45.5 us
    gather x1, local copies, waits for them, and re-layouts, shards(): doc_weights[ranking]  45.5 us
    dot_general x8, matrix products, per_bunch(): jnp.einsum('gdb,dk->gkb', one_hot, spread, preferred_element_type=jnp.flo...  35 us
    gather x2, local copies, waits for them, and re-layouts, shards(): outgoing = owner_stats[:, slot_in]  31.8 us
    scatter x1, local copies, waits for them, and re-layouts, shards(): owner_values = jnp.zeros((2, doc_count), jnp.float32).at[:, slot_in.resha...  23 us
    scatter x1, local copies, waits for them, and re-layouts, shards(): jnp.zeros((2, doc_count), jnp.bfloat16).at[:, ranking]  22.1 us
  transfers between devices with their start and end apart: 4, of which 3 were waited for; matrix products, arithmetic and copies ran while one was open for 16% of the time, Pallas kernels for 0%

profile of v1, /device:TPU:2, one launch (start us, length us, event | category | flops | bytes accessed | tf_op | source)
XLA Modules:
  0.0 601.9 jit_solution(1001898832791064327)
XLA Ops:
  6.5 7.6 %sort.17 = (s32[8192]{0:T(1024)}, s32[8192]{0:T(1024)S(1)}) sort(s32[8192]{0:T(1024)} %param.15, s32[8192]{0:T(1024)S(1)} %iota.15), dimensions={0}, to_apply=%region_0.0 | sort | flops 106496 | bytes 131072 | tf_op jit(solution)/shard_map/jit(argsort)/sort | solution.py:51
  14.2 45.5 %gather_fusion = s32[8192]{0:T(1024)S(1)} fusion(s32[8192]{0:T(1024)S(1)} %copy-done.1, s32[8192]{0:T(1024)S(1)} %get-tuple-element.140), kind=kCustom, calls=%fused_computation | custom fusion | bytes 98304 | tf_op jit(solution)/shard_map/gather | solution.py:52
  60.4 7.5 %all-to-all-start = ((s32[16,1,512]{2,1,0:T(1,128)}), s32[16,1,512]{2,1,0:T(1,128)S(1)}, u32[]{:S(2)}, u32[]{:S(2)}) async-start(s32[16,1,512]{2,1,0:T(1,128)} %and_select_fusion), calls=%async_computation | async-start | bytes 65536 | tf_op jit(solution)/shard_map/all_to_all | solution.py:56
  67.9 45.5 %gather_fusion.1 = f32[8192]{0:T(1024)S(1)} fusion(f32[8192]{0:T(1024)S(1)} %copy-done, s32[8192]{0:T(1024)S(1)} %get-tuple-element.140), kind=kCustom, calls=%fused_computation.1 | custom fusion | bytes 98304 | tf_op jit(solution)/shard_map/gather | solution.py:53
  114.2 45.5 %gather_fusion.2 = f32[8192]{0:T(1024)S(1)} fusion(f32[8192]{0:T(1024)S(1)} %copy-done.2, s32[8192]{0:T(1024)S(1)} %get-tuple-element.140), kind=kCustom, calls=%fused_computation.2 | custom fusion | bytes 98304 | tf_op jit(solution)/shard_map/gather | solution.py:53
  160.5 7.2 %all-to-all-start.1 = ((f32[2,16,512]{2,0,1:T(2,128)}), f32[2,16,512]{2,0,1:T(2,128)S(1)}, u32[]{:S(2)}, u32[]{:S(2)}) async-start(f32[2,16,512]{2,0,1:T(2,128)} %copy.31), calls=%async_computation.1 | async-start | bytes 131072 | tf_op jit(solution)/shard_map/all_to_all | solution.py:55
  167.9 6.2 %all-to-all-done.1 = f32[2,16,512]{2,0,1:T(2,128)S(1)} async-done(((f32[2,16,512]{2,0,1:T(2,128)}), f32[2,16,512]{2,0,1:T(2,128)S(1)}, u32[]{:S(2)}, u32[]{:S(2)}) %all-to-all-start.1) | async-done | bytes 65568 | tf_op jit(solution)/shard_map/all_to_all | solution.py:55
  176.7 23.0 %scatter_custom_fusion = f32[2,8192]{0,1:T(8,128)} fusion(s32[8192]{0:T(1024)S(1)} %bitcast.109, f32[8192,2]{1,0:T(8,128)} %copy.32, f32[]{:T(128)} %constant.40.clone.1), kind=kCustom, calls=%fused_computation.44 | custom fusion | bytes 66048 | tf_op jit(solution)/shard_map/scatter | solution.py:60
  199.7 6.8 %slice_reduce_fusion = (f32[8192]{0:T(1024)S(1)}, f32[8192]{0:T(1024)S(1)}) fusion(f32[2,8192]{0,1:T(8,128)} %scatter_custom_fusion), kind=kLoop, calls=%fused_computation.42 | loop fusion | bytes 131072 | tf_op jit(solution)/shard_map/slice | solution.py:62
  206.5 18.5 %while.23 = (s32[]{:T(128)}, bf16[16,2,256]{2,1,0:T(2,128)(2,1)S(1)}, bf16[16,2,256]{2,1,0:T(2,128)(2,1)S(1)}, f32[16,2,256]{2,1,0:T(2,128)S(1)}, f32[16,2,256]{...) while((s32[]{:T(128)}, bf16[16,2,256]{2,1,0:T(2,128)(2,1)S(1)}, ...), condition=%wide.region_4.5_spmd, body=%wide.region_2.4_spmd.sunk | while | flops 3806722 | bytes 57449 | solution.py:41
  226.3 29.2 %gather_fusion.3 = bf16[8192,2]{1,0:T(8,128)(2,1)} fusion(bf16[2,8192]{0,1:T(8,128)(2,1)S(1)} %copy.33, s32[8192]{0:T(1024)S(1)} %broadcast_clamp_fusion), kind=kCustom, calls=%fused_computation.3 | custom fusion | bytes 98304 | tf_op jit(solution)/shard_map/gather | solution.py:63
  258.2 4.7 all-to-all-start.2
  264.5 4.7 all-to-all-done.2
  271.1 22.1 %scatter_custom_fusion.1 = bf16[2,8192]{0,1:T(8,128)(2,1)S(1)} fusion(s32[8192]{0:T(1024)S(1)} %get-tuple-element.141, bf16[8192,2]{1,0:T(8,128)(2,1)} %copy.35, bf16[]{:T(256)} %constant.56.clone.1), kind=kCustom, calls=%fused_computation.48 | custom fusion | bytes 33280 | tf_op jit(solution)/shard_map/scatter | solution.py:66
  294.1 85.1 %while.24 = (s32[]{:T(128)}, f32[8,4,128,128]{3,2,1,0:T(8,128)}, s32[8,4,8192]{2,1,0:T(4,128)}, bf16[8192,2]{0,1:T(2,128)(2,1)S(1)}, bf16[8192,64]{0,1:T(8,128)(2,1)S(1)}, /*index=5*/s32[]{:T(128)}) while((s32[]{:T(128)}, f32[8,4,128,128]{3,2,1,0:T(8,128)}, s32[8,4,8192]{2,1,0:T(4,128)}, bf16[8192,2]{0,1:T(2,128)(2,1)S(1)}, ...), condition=%wide.region_7.8_spmd.clone, body=%wide.region_6.7_spmd.clone.sunk | while | flops 1078984704 | bytes 11174473 | solution.py:83
  299.5 4.4 fusion.47
  310.2 4.4 fusion.47
  320.8 4.4 fusion.47
  331.4 4.4 fusion.47
  352.7 4.4 fusion.47
  363.3 4.4 fusion.47
  373.9 4.4 fusion.47
  379.2 202.3 %all-gather.3.cloned.1.call-done = f32[1024,32,2,128]{3,2,0,1:T(2,128)} async-done(((f32[64,32,2,128]{3,2,0,1:T(2,128)}), f32[1024,32,2,128]{3,2,0,1:T(2,128)}) %all-gather.3.cloned.1.call-update) | async-done | bytes 33554448 | tf_op jit(solution)/shard_map/all_gather | solution.py:13
  581.5 12.8 %reduce_sum.9 = f32[64,32,2,128]{3,2,0,1:T(2,128)S(1)} reduce(f32[16,64,32,2,128]{4,3,1,0,2:T(2,128)} %bitcast.99, f32[]{:T(128)} %constant.40.clone.1), dimensions={0}, to_apply=%region_8.9 | reduce | flops 7864320 | bytes 35651588 | tf_op jit(solution)/shard_map/reduce_sum | solution.py:14
  (216 shorter events, 85.8 us)
Async XLA Ops:
  6.5 61.3 %copy-start = (f32[8192]{0:T(1024)S(1)}, f32[8192]{0:T(1024)}, u32[]{:S(2)}) copy-start(f32[8192]{0:T(1024)} %param.13) | copy-start | bytes 98308
  6.5 7.6 %copy-start.1 = (s32[8192]{0:T(1024)S(1)}, s32[8192]{0:T(1024)}, u32[]{:S(2)}) copy-start(s32[8192]{0:T(1024)} %param.15) | copy-start | bytes 98308
  60.4 100.1 %all-to-all-start = ((s32[16,1,512]{2,1,0:T(1,128)}), s32[16,1,512]{2,1,0:T(1,128)S(1)}, u32[]{:S(2)}, u32[]{:S(2)}) async-start(s32[16,1,512]{2,1,0:T(1,128)} %and_select_fusion), calls=%async_computation | async-start | bytes 65536 | tf_op jit(solution)/shard_map/all_to_all | solution.py:56
  113.4 0.8 copy-start.2
  114.2 46.3 %copy-start.5 = (s32[8192]{0:T(1024)S(1)}, s32[8192]{0:T(1024)}, u32[]{:S(2)}) copy-start(s32[8192]{0:T(1024)} %param.17) | copy-start | bytes 98308
  114.2 46.3 %copy-start.6 = (s32[8192]{0:T(1024)S(1)}, s32[8192]{0:T(1024)}, u32[]{:S(2)}) copy-start(s32[8192]{0:T(1024)} %param.16) | copy-start | bytes 98308
  160.5 13.5 %all-to-all-start.1 = ((f32[2,16,512]{2,0,1:T(2,128)}), f32[2,16,512]{2,0,1:T(2,128)S(1)}, u32[]{:S(2)}, u32[]{:S(2)}) async-start(f32[2,16,512]{2,0,1:T(2,128)} %copy.31), calls=%async_computation.1 | async-start | bytes 131072 | tf_op jit(solution)/shard_map/all_to_all | solution.py:55
  225.2 37.7 %copy-start.4 = (s32[8192]{0:T(1024)S(1)}, s32[8192]{0:T(1024)}, u32[]{:S(2)}) copy-start(s32[8192]{0:T(1024)} %param.12) | copy-start | bytes 98308
  226.3 36.9 %copy-start.3 = (s32[32,8192]{1,0:T(8,128)S(1)}, s32[32,8192]{1,0:T(8,128)}, u32[]{:S(2)}) copy-start(s32[32,8192]{1,0:T(8,128)} %param.11) | copy-start | bytes 3145732
  258.2 11.0 %all-to-all-start.2 = ((bf16[2,16,512]{2,0,1:T(2,128)(2,1)}), bf16[2,16,512]{2,0,1:T(2,128)(2,1)S(1)}, u32[]{:S(2)}, u32[]{:S(2)}) async-start(bf16[2,16,512]{2,0,1:T(2,128)(2,1)} %bitcast.18), calls=%async_computation.2 | async-start | bytes 65536 | tf_op jit(solution)/shard_map/all_to_all | solution.py:64
  262.9 318.6 %all-gather.3.cloned.1.call-start = ((), (), s32[]{:S(2)}) async-start(), calls=%async_computation.3 | async-start | bytes 35651584 | tf_op jit(solution)/shard_map/all_gather | solution.py:13
Sparse Core Ops, SparseCore 0:
  379.3 202.1 all-gather.2
